TPU v7x, 512 devices: a whole 4x4x16 slice. The times are simulated.
512 devices in a mesh: prow: 32 (over z, core), pcol: 16 (over x, y).
Axes of the slice: x: 4, y: 4, z: 16, core: 2. Of those that a mesh axis runs over, the one named last changes fastest.
Arguments:
- trailing: bfloat16 [8, 8192, 2, 4096], P(None, 'prow', None, 'pcol'), may hold values from -6 to 6
- panel: bfloat16 [256, 8, 8192], P('pcol', None, 'prow'), may hold values from -1 to 1
- lower_inverse: bfloat16 [256, 256], replicated
- upper_inverse: bfloat16 [256, 256], replicated
- pivots: int32 [256], replicated, may hold values from 0 to 65535, as said below
Outputs:
- updated: bfloat16 [8, 8192, 2, 4096], P(None, 'prow', None, 'pcol')
Inputs may be any that keep to these rules, and one draw needn't show every extreme that they name: `pivots`: the entries are distinct; entry i is either i or a row index of 256 or more. Entry 0 is 0 and entry 1 is 65535.
All inputs are finite; a program needn't handle non-finite values.
Results may differ from a plain program's by a relative error of at most 0.0054.
Values may be sent and summed in bfloat16 or wider, within the bound.
A program may use at most 64 MiB of HBM per device.

v0:
```python
import jax
import jax.numpy as jnp
from jax import lax
from jax.sharding import PartitionSpec as P


def from_root(x, axis, root):
    mine = lax.axis_index(axis) == root
    return lax.psum(jnp.where(mine, x, jnp.zeros_like(x)), axis)


def contract_lead(left_side, right_side):
    return lax.dot_general(
        left_side, right_side, (((0,), (0,)), ((), ())), preferred_element_type=jnp.float32
    )


def per_device(trailing, panel, lower_inverse, upper_inverse, pivots):
    row_blocks, block_size, col_blocks, col_size = trailing.shape
    local_rows = row_blocks * block_size
    matrix = trailing.reshape(local_rows, col_blocks * col_size)
    panel_rows = panel.reshape(panel.shape[0], local_rows)
    prow_count = lax.axis_size("prow")
    prow_index = lax.axis_index("prow")
    head_rows = jnp.arange(block_size, dtype=jnp.int32)
    pivot_owner = pivots // block_size % prow_count
    pivot_local = pivots // (block_size * prow_count) * block_size + pivots % block_size
    pivot_here = pivot_owner == prow_index
    fetched = jnp.take(matrix, jnp.where(pivot_here, pivot_local, 0), axis=0)
    picked = jnp.where(pivot_here[:, None], fetched, jnp.zeros_like(fetched))
    old_top = matrix[:block_size]
    at_root = prow_index == 0
    source = picked[None]
    gathered_top = lax.psum(source, "prow").astype(jnp.float32).astype(jnp.bfloat16)
    solved = jnp.dot(lower_inverse, gathered_top[0], preferred_element_type=jnp.float32).astype(
        jnp.bfloat16
    )
    root_top = from_root(old_top, "prow", 0)
    local_index = jnp.arange(local_rows, dtype=jnp.int32)
    global_rows = (
        local_index // block_size * prow_count + prow_index
    ) * block_size + local_index % block_size
    matches = (global_rows[:, None] == pivots[None, :]) & (pivots != head_rows)[None, :]
    incoming = jnp.sum(jnp.where(matches, head_rows[None, :], 0), axis=1)
    has_incoming = jnp.any(matches, axis=1)
    swapped = jnp.where(has_incoming[:, None], jnp.take(root_top, incoming, axis=0), matrix)
    lower_t = contract_lead(upper_inverse, lax.all_gather(panel_rows, "pcol", axis=0, tiled=True))
    lower_t = lower_t.astype(jnp.bfloat16)
    product = contract_lead(lower_t, solved)
    updated = (swapped.astype(jnp.float32) - product).astype(jnp.bfloat16)
    top_block = jnp.where(at_root, solved, updated[:block_size])
    updated = lax.dynamic_update_slice_in_dim(updated, top_block, 0, 0)
    return updated.reshape(trailing.shape)


def solution(mesh):
    placed = (P(None, "prow", None, "pcol"), P("pcol", None, "prow"), P(), P(), P())
    return jax.shard_map(
        per_device,
        mesh=mesh,
        in_specs=placed,
        out_specs=P(None, "prow", None, "pcol"),
        check_vma=False,
    )
```

profile of v0, /device:TPU:1, one launch (start us, length us, event | category | flops | bytes accessed | tf_op | source)
XLA Modules:
  0.0 261.1 jit_solution(12199682226288083791)
XLA Ops:
  7.4 0.0 copy-start
  7.4 0.0 all-reduce.3.cloned.1.call-start
  7.4 0.7 compare_and_fusion.2
  8.1 1.2 broadcast_select_fusion
  9.3 0.7 copy.23
  10.0 2.0 copy.24
  12.1 0.0 copy-start.4
  12.1 1.2 gather_fusion.1
  13.2 0.8 fusion.3
  14.1 0.0 all-reduce.3.cloned.1.call-update
  14.1 0.0 all-gather.2.cloned.1.call-start
  14.1 0.0 copy-done.4
  14.2 0.6 copy.25
  14.8 0.0 all-gather.2.cloned.1.call-update
  14.8 0.0 copy-start.5
  14.8 2.4 copy.22
  17.2 0.0 copy-done.5
  17.2 0.8 fusion
  18.0 0.9 select_reduce_fusion
  18.9 212.9 %all-reduce.3.cloned.1.call-done = (bf16[256,512]{1,0:T(8,128)(2,1)}, bf16[256,512]{1,0:T(8,128)(2,1)}) async-done(((bf16[256,512]{1,0:T(8,128)(2,1)}, bf16[256,512]{1,0:T(8,128)(2,1)}), (bf16[256,512]{1,0:T(8,128)(2,1)}, bf16[256,512]{1,0:T(8,128)(2,1)})) %all-reduce.3.cloned.1.call-update) | async-done | bytes 524304 | tf_op jit(solution)/shard_map/psum | solution.py:34
  231.8 8.6 %gather_fusion = bf16[2048,512]{1,0:T(8,128)(2,1)S(1)} fusion(bf16[256,512]{1,0:T(8,128)(2,1)} %get-tuple-element.6, s32[2048]{0:T(1024)S(1)} %broadcast_clamp_fusion), kind=kCustom, calls=%fused_computation | custom fusion | bytes 4202496 | tf_op jit(solution)/shard_map/jit(_take)/gather | solution.py:46
  240.4 0.0 copy-start.2
  240.4 0.0 copy-start.3
  240.4 2.5 copy.16
  242.8 0.0 copy-done.2
  242.8 0.0 copy-done.3
  242.8 0.3 convolution_convert_fusion.1
  243.1 0.0 all-gather.2.cloned.1.call-done
  243.1 0.0 copy-done
  243.2 3.8 %subtract_convert_fusion = bf16[2048,512]{0,1:T(8,128)(2,1)S(1)} fusion(bf16[512,256]{1,0:T(8,128)(2,1)S(1)} %convolution_convert_fusion.1, bf16[2048,512]{0,1:T(8,128)(2,1)} %copy.22, bf16[2048,512]{0,1:T(8,128)(2,1)} %copy.16, pred[2048]{0:T(1024)(128)(4,1)S(1)} %compare_and_fusion.1, pred[2048]{0:T(1024)(128)(4,1)S(1)} %fusion, ...), kind=kOutput, calls=%fused_computation.2 | convolution fusion | flops 811073536 | bytes 7737344 | tf_op jit(solution)/shard_map/dot_general | solution.py:13
  246.9 0.1 fusion.1
  247.1 0.0 copy-start.1
  247.1 1.3 copy-done.1
  248.4 2.3 copy.26
  250.7 3.0 %copy.20 = bf16[8,256,2,256]{3,2,1,0:T(2,128)(2,1)} copy(bf16[8,256,2,256]{1,0,3,2:T(8,128)(2,1)S(1)} %bitcast.32) | data formatting | bytes 4194304 | tf_op jit(solution)/shard_map/reshape | solution.py:53
  (5 shorter events, 0.0 us)
Async XLA Ops:
  7.4 235.8 %copy-start = (bf16[256,256]{1,0:T(8,128)(2,1)S(1)}, bf16[256,256]{1,0:T(8,128)(2,1)}, u32[]{:S(2)}) copy-start(bf16[256,256]{1,0:T(8,128)(2,1)} %param.8) | copy-start | bytes 393220
  7.4 224.4 %all-reduce.3.cloned.1.call-start = ((), (), s32[]{:S(2)}) async-start(), calls=%async_computation.1 | async-start | bytes 1048576 | tf_op jit(solution)/shard_map/psum | solution.py:34
  12.1 2.1 copy-start.4
  14.1 229.0 %all-gather.2.cloned.1.call-start = ((), (), s32[]{:S(2)}) async-start(), calls=%async_computation | async-start | bytes 1114112 | tf_op jit(solution)/shard_map/all_gather | solution.py:47
  14.8 2.4 copy-start.5
  240.4 2.5 copy-start.2
  240.4 2.5 copy-start.3
  247.1 1.3 copy-start.1
Sparse Core Ops, SparseCore 0:
  14.2 217.5 all-reduce.2
Sparse Core Ops, SparseCore 1:
  17.6 61.1 all-gather.1
where the time goes:
time: 261 us
  waiting for transfers between devices  213 us (82%)
  local copies, waits for them, and re-layouts  24.5 us (9%)
  between operations  15 us (6%)
  other arithmetic  4.52 us (2%)
  matrix products  4.05 us (2%)
    psum x1, waiting for transfers between devices, per_device(): lax.psum(source, 'prow').astype(jnp.float32).astype(jnp.bfloat16)  213 us
    gather x2, local copies, waits for them, and re-layouts, per_device(): jnp.take(root_top, incoming, axis=0)  11 us
    unnamed x16, local copies, waits for them, and re-layouts  7.01 us
  transfers between devices with their start and end apart: 2, of which 1 were waited for; matrix products, arithmetic and copies ran while one was open for 6% of the time, Pallas kernels for 0%

commit v1 on v0

--- a/solution.py
+++ b/solution.py
@@ -31,7 +31,9 @@
     old_top = matrix[:block_size]
     at_root = prow_index == 0
     source = picked[None]
-    gathered_top = lax.psum(source, "prow").astype(jnp.float32).astype(jnp.bfloat16)
+    gathered_top = (
+        jnp.sum(lax.all_gather(source, "prow"), axis=0).astype(jnp.float32).astype(jnp.bfloat16)
+    )
     solved = jnp.dot(lower_inverse, gathered_top[0], preferred_element_type=jnp.float32).astype(
         jnp.bfloat16
     )

time: 261 us -> 380 us (1.46)
  waiting for transfers between devices: 213 us -> 328 us
  other arithmetic: 4.52 us -> 9.26 us
    all_gather x0 -> x1, waiting for transfers between devices: none -> 70.1 us  [per_device(): lax.all_gather(source, 'prow')]
    all_gather x1, waiting for transfers between devices: 0.03 us -> 50.2 us  [per_device(): lax.all_gather(panel_rows, 'pcol', axis=0, tiled=True)]
    psum x1, waiting for transfers between devices: 213 us -> 207 us  [from_root(): return lax.psum(jnp.where(mine, x, jnp.zeros_like(x)), axis)]
    reduce_sum x0 -> x1, other arithmetic: none -> 4.75 us  [per_device(): jnp.sum(lax.all_gather(source, 'prow'), axis=0).astype(jnp.float32)]
  transfers between devices with their start and end apart: 2 -> 3, of which waited for: 1 -> 3; matrix products, arithmetic and copies ran while one was open for 6% -> 7% of each run, Pallas kernels for 0% -> 0%
where the time goes in v1:
time: 380 us; the launch traced here: 379 us
  waiting for transfers between devices  328 us (86%)
  local copies, waits for them, and re-layouts  24.6 us (6%)
  between operations  13.2 us (3%)
  other arithmetic  9.26 us (2%)
  matrix products  3.99 us (1%)
    psum x1, waiting for transfers between devices, from_root(): return lax.psum(jnp.where(mine, x, jnp.zeros_like(x)), axis)  207 us
    all_gather x1, waiting for transfers between devices, per_device(): lax.all_gather(source, 'prow')  70.1 us
    all_gather x1, waiting for transfers between devices, per_device(): lax.all_gather(panel_rows, 'pcol', axis=0, tiled=True)  50.2 us
    gather x2, local copies, waits for them, and re-layouts, per_device(): jnp.take(root_top, incoming, axis=0)  11.1 us
  transfers between devices with their start and end apart: 3, of which 3 were waited for; matrix products, arithmetic and copies ran while one was open for 7% of the time, Pallas kernels for 0%

profile of v1, /device:TPU:1, one launch (start us, length us, event | category | flops | bytes accessed | tf_op | source)
XLA Modules:
  0.0 378.8 jit_solution(18030564050243366710)
XLA Ops:
  6.5 0.0 copy-start
  6.5 0.0 all-reduce.2.cloned.1.call-start
  6.5 1.2 broadcast_select_fusion
  7.7 0.7 copy.28
  8.5 0.0 all-reduce.2.cloned.1.call-update
  8.5 0.0 all-gather.5.cloned.1.call-start
  8.6 0.7 compare_and_fusion.2
  9.3 2.0 copy.29
  11.3 0.0 copy-start.3
  11.3 1.2 gather_fusion.1
  12.5 0.8 fusion.2
  13.3 0.0 all-gather.5.cloned.1.call-update
  13.3 0.0 all-gather.3.cloned.1.call-start
  13.4 0.0 copy-done.3
  13.4 0.6 copy.30
  14.0 0.0 all-gather.3.cloned.1.call-update
  14.1 0.0 copy-start.4
  14.1 2.4 copy.27
  16.5 0.0 copy-done.4
  16.5 0.7 fusion
  17.2 0.9 select_reduce_fusion
  18.1 207.3 %all-reduce.2.cloned.1.call-done = bf16[256,512]{1,0:T(8,128)(2,1)} async-done(((bf16[256,512]{1,0:T(8,128)(2,1)}), bf16[256,512]{1,0:T(8,128)(2,1)}) %all-reduce.2.cloned.1.call-update) | async-done | bytes 262160 | tf_op jit(solution)/shard_map/psum | solution.py:9
  225.5 8.6 %gather_fusion = bf16[2048,512]{1,0:T(8,128)(2,1)S(1)} fusion(bf16[256,512]{1,0:T(8,128)(2,1)} %all-reduce.2.cloned.1.call-done, s32[2048]{0:T(1024)S(1)} %broadcast_clamp_fusion), kind=kCustom, calls=%fused_computation | custom fusion | bytes 4202496 | tf_op jit(solution)/shard_map/jit(_take)/gather | solution.py:48
  234.0 2.5 copy.21
  236.5 0.0 copy-start.2
  236.5 70.1 %all-gather.5.cloned.1.call-done = bf16[32,1,256,512]{3,2,1,0:T(8,128)(2,1)} async-done(((bf16[1,1,256,512]{3,2,1,0:T(8,128)(2,1)}), bf16[32,1,256,512]{3,2,1,0:T(8,128)(2,1)}) %all-gather.5.cloned.1.call-update) | async-done | bytes 8388624 | tf_op jit(solution)/shard_map/all_gather | solution.py:35
  306.6 4.8 %reduce_sum.25 = bf16[256,512]{1,0:T(8,128)(2,1)S(1)} reduce(bf16[32,1,256,512]{3,2,1,0:T(8,128)(2,1)} %all-gather.5.cloned.1.call-done, bf16[]{:T(256)} %constant.106.clone.1), dimensions={0,1}, to_apply=%region_3.4 | reduce | flops 4063232 | bytes 8650754 | tf_op jit(solution)/shard_map/reduce_sum | solution.py:35
  311.4 0.0 copy-done.2
  311.4 0.3 convolution_convert_fusion.1
  311.6 50.2 %all-gather.3.cloned.1.call-done = bf16[256,2048]{1,0:T(8,128)(2,1)} async-done(((bf16[16,2048]{1,0:T(8,128)(2,1)}), bf16[256,2048]{1,0:T(8,128)(2,1)}) %all-gather.3.cloned.1.call-update) | async-done | bytes 1048592 | tf_op jit(solution)/shard_map/all_gather | solution.py:49
  361.8 0.0 copy-done
  361.8 3.7 subtract_convert_fusion
  365.6 0.1 fusion.1
  365.7 0.0 copy-start.1
  365.7 1.3 copy-done.1
  367.0 2.3 copy.31
  369.3 3.0 copy.25
  (5 shorter events, 0.0 us)
Async XLA Ops:
  6.5 355.3 %copy-start = (bf16[256,256]{1,0:T(8,128)(2,1)S(1)}, bf16[256,256]{1,0:T(8,128)(2,1)}, u32[]{:S(2)}) copy-start(bf16[256,256]{1,0:T(8,128)(2,1)} %param.8) | copy-start | bytes 393220
  6.5 218.9 %all-reduce.2.cloned.1.call-start = ((), (), s32[]{:S(2)}) async-start(), calls=%async_computation | async-start | bytes 524288 | tf_op jit(solution)/shard_map/psum | solution.py:9
  8.5 298.1 %all-gather.5.cloned.1.call-start = ((), (), s32[]{:S(2)}) async-start(), calls=%async_computation.2 | async-start | bytes 8650752 | tf_op jit(solution)/shard_map/all_gather | solution.py:35
  11.3 2.1 copy-start.3
  13.3 348.5 %all-gather.3.cloned.1.call-start = ((), (), s32[]{:S(2)}) async-start(), calls=%async_computation.1 | async-start | bytes 1114112 | tf_op jit(solution)/shard_map/all_gather | solution.py:49
  14.1 2.4 copy-start.4
  236.5 74.8 %copy-start.2 = (bf16[256,256]{1,0:T(8,128)(2,1)S(1)}, bf16[256,256]{1,0:T(8,128)(2,1)}, u32[]{:S(2)}) copy-start(bf16[256,256]{1,0:T(8,128)(2,1)} %param.7) | copy-start | bytes 393220
  365.7 1.3 copy-start.1
Sparse Core Ops, SparseCore 0:
  9.6 215.7 all-reduce.1
  227.6 78.9 all-gather.4
  309.6 52.1 all-gather.2
